TPU v7x, 256 devices: a whole 4x4x8 slice. The times are simulated.
256 devices in a mesh: seq: 8 (over z), head: 4 (over y_hi, core), rep: 8 (over y_lo, x).
Axes of the slice: x: 4, y: 4 (y_hi: 2, y_lo: 2; y = y_hi * 2 + y_lo), z: 8, core: 2. Of those that a mesh axis runs over, the one named last changes fastest.
Arguments:
- queries: bfloat16 [8, 2048, 7168], P('rep', 'seq', 'head'), may hold values from -6 to 6
- new_keys: bfloat16 [8, 2048, 7168], P('rep', 'seq', 'head'), may hold values from -6 to 6
- new_values: bfloat16 [8, 2048, 7168], P('rep', 'seq', 'head'), may hold values from -4 to 4
- lengths: int32 [8, 4], P('rep'), may hold values from 1 to 1024, 2048 in all within a row
- offsets: int32 [8, 4], P('rep'), may hold values from 0 to 4095
- slot_map: int32 [8, 4], P('rep'), may hold values from 0 to 3, each once within a row
Outputs:
- attended: bfloat16 [8, 2048, 7168], P('rep', 'seq', 'head')
- key_cache: bfloat16 [8, 4, 1024, 7168], P('rep', 'head', None, 'seq')
- value_cache: bfloat16 [8, 4, 1024, 7168], P('rep', 'head', None, 'seq')
Inputs may be any that keep to these rules, and one draw needn't show every extreme that they name: `lengths`: each row sums to 2048; its first entry is the group's shared prompt; every row has one entry equal to 1024. `slot_map`: each row is a permutation of the group's requests.
All inputs are finite; a program needn't handle non-finite values.
Results may differ from a plain program's by a relative error of at most 0.011.
Values may be sent and summed in bfloat16 or wider, within the bound.
A program may use at most 128 MiB of HBM per device.

v0:
```python
import math
import jax
import jax.numpy as jnp
from jax import lax
from jax.sharding import PartitionSpec as P

HD = 224
NEG_FILL = -1e30
ROPE_BASE = 10000.0
KEY_BLOCK = 512


def rotate(source, places):
    full_width = source.shape[-1]
    half_width = full_width // 2
    inverse = jnp.power(
        jnp.float32(ROPE_BASE), -2.0 * jnp.arange(half_width, dtype=jnp.float32) / full_width
    )
    angles = places.astype(jnp.float32)[:, None] * inverse[None, :]
    cosine = jnp.cos(angles)[:, None, :]
    sine_terms = jnp.sin(angles)[:, None, :]
    first_part = source[..., :half_width].astype(jnp.float32)
    second_part = source[..., half_width:].astype(jnp.float32)
    rotated = jnp.concatenate(
        [
            first_part * cosine - second_part * sine_terms,
            second_part * cosine + first_part * sine_terms,
        ],
        axis=-1,
    )
    return rotated.astype(jnp.bfloat16)


def token_request(token_ids, ends_at):
    return jnp.sum((token_ids[:, None] >= ends_at[None, :]).astype(jnp.int32), axis=1)


def lookup_rows(request, lookup):
    matches = request[:, None] == jnp.arange(lookup.shape[0], dtype=jnp.int32)[None, :]
    return jnp.sum(jnp.where(matches, lookup[None, :], 0), axis=1)


def empty_state(head_count, row_count):
    return (
        jnp.full((head_count, row_count), NEG_FILL, jnp.float32),
        jnp.zeros((head_count, row_count), jnp.float32),
        jnp.zeros((head_count, row_count, HD), jnp.float32),
    )


def finish(running):
    row_best, row_total, summed = running
    head_count, row_count, _ = summed.shape
    return (
        (summed / row_total[:, :, None])
        .transpose(1, 0, 2)
        .reshape(row_count, head_count * HD)
        .astype(jnp.bfloat16)
    )


def update(
    running, query_token_rows, query_tok, query_req, key_rows, value_rows, key_start, ends_at
):
    row_count = key_rows.shape[0]
    head_count = query_token_rows.shape[1]
    key_token_index = key_start + jnp.arange(row_count, dtype=jnp.int32)
    key_req = token_request(key_token_index, ends_at)
    same_request = (key_req[None, :] == query_req[:, None]) & (
        key_token_index[None, :] <= query_tok[:, None]
    )
    prompt_keys = (key_req[None, :] == 0) & (query_req[:, None] != 0)
    allowed = same_request | prompt_keys
    row_best, row_total, summed = running
    key_head_stack = key_rows.reshape(row_count, head_count, HD)
    value_heads = value_rows.reshape(row_count, head_count, HD)
    scores = jnp.einsum(
        "ezq,izq->zei", query_token_rows, key_head_stack, preferred_element_type=jnp.float32
    ) * (1.0 / math.sqrt(HD))
    scores = jnp.where(allowed[None], scores, NEG_FILL)
    best_new = jnp.maximum(row_best, jnp.max(scores, axis=2))
    factor = jnp.exp(row_best - best_new)
    weights = jnp.where(allowed[None], jnp.exp(scores - best_new[:, :, None]), 0.0)
    total_new = row_total * factor + jnp.sum(weights, axis=2)
    mixed = jnp.einsum(
        "eva,ael->evl",
        weights.astype(jnp.bfloat16),
        value_heads,
        preferred_element_type=jnp.float32,
    )
    return (best_new, total_new, summed * factor[:, :, None] + mixed)


def per_device(queries, new_keys, new_values, lengths, offsets, slot_map):
    tok_dev = queries.shape[1]
    local_cols = queries.shape[2]
    head_count = local_cols // HD
    tokens_total = tok_dev * lax.axis_size("seq")
    cache_len = tokens_total // 2
    lengths_row = lengths[0]
    offsets_row = offsets[0]
    slots_row = slot_map[0]
    request_count = lengths_row.shape[0]
    ends_at = jnp.cumsum(lengths_row)
    begins = ends_at - lengths_row
    token_ids = lax.axis_index("seq") * tok_dev + jnp.arange(tok_dev, dtype=jnp.int32)
    request = token_request(token_ids, ends_at)
    places = lookup_rows(request, offsets_row) + token_ids - lookup_rows(request, begins)
    rot_queries = rotate(queries[0].reshape(tok_dev, head_count, HD), places)
    rot_keys = rotate(new_keys[0].reshape(tok_dev, head_count, HD), places).reshape(
        tok_dev, local_cols
    )
    value_rows = new_values[0]
    key_rows = lax.all_gather(rot_keys, "seq", axis=0, tiled=True)
    piece_values = lax.all_gather(value_rows, "seq", axis=0, tiled=True)
    row_count = key_rows.shape[0]

    def key_step(key_index, state_in):
        first_row = key_index * KEY_BLOCK
        return update(
            state_in,
            rot_queries,
            token_ids,
            request,
            lax.dynamic_slice_in_dim(key_rows, first_row, KEY_BLOCK, 0),
            lax.dynamic_slice_in_dim(piece_values, first_row, KEY_BLOCK, 0),
            first_row,
            ends_at,
        )

    finished = lax.fori_loop(0, row_count // KEY_BLOCK, key_step, empty_state(head_count, tok_dev))
    attended = finish(finished)
    stacked = jnp.stack([rot_keys, value_rows])
    my_slot = lax.axis_index("head")
    request_ids = jnp.arange(request_count, dtype=jnp.int32)
    owner = jnp.sum(jnp.where(slots_row == my_slot, request_ids, 0))
    owner_begin = jnp.sum(jnp.where(request_ids == owner, begins, 0))
    slot_of = lookup_rows(request, slots_row)
    member = slot_of[None, :] == request_ids[:, None]
    buckets = jnp.where(member[None, :, :, None], stacked[:, None], jnp.zeros((), jnp.bfloat16))
    moved = lax.all_to_all(
        lax.all_to_all(buckets, "head", split_axis=1, concat_axis=3, tiled=True),
        "seq",
        split_axis=3,
        concat_axis=2,
        tiled=True,
    )
    padded = jnp.concatenate(
        [moved, jnp.zeros((2, 1, cache_len, moved.shape[3]), jnp.bfloat16)], axis=2
    )
    window = lax.dynamic_slice_in_dim(padded, owner_begin, cache_len, 2)
    return (attended[None], window[0:1], window[1:2])


def solution(mesh):
    in_specs = (
        P("rep", "seq", "head"),
        P("rep", "seq", "head"),
        P("rep", "seq", "head"),
        P("rep", None),
        P("rep", None),
        P("rep", None),
    )
    out_specs = (
        P("rep", "seq", "head"),
        P("rep", "head", None, "seq"),
        P("rep", "head", None, "seq"),
    )
    return jax.shard_map(
        per_device, mesh=mesh, in_specs=in_specs, out_specs=out_specs, check_vma=False
    )
```

profile of v0, /device:TPU:96, one launch (start us, length us, event | category | flops | bytes accessed | tf_op | source)
XLA Modules:
  0.0 385.8 jit_solution(3452643616625133445)
XLA Ops:
  8.8 1.5 copy.46
  14.9 1.4 pad_maximum_fusion
  16.3 2.8 copy.50
  19.1 3.4 broadcast_select_fusion
  22.6 5.6 %all-to-all-start = ((bf16[2,4,256,1792]{2,3,0,1:T(8,128)(2,1)}), bf16[2,4,256,1792]{2,3,0,1:T(8,128)(2,1)}, u32[]{:S(2)}, u32[]{:S(2)}) async-start(bf16[2,4,256,1792]{2,3,0,1:T(8,128)(2,1)} %broadcast_select_fusion), calls=%async_computation | async-start | bytes 14680064 | tf_op jit(solution)/shard_map/all_to_all | solution.py:142
  33.0 78.6 %all-to-all-done = bf16[2,4,256,1792]{2,3,0,1:T(8,128)(2,1)} async-done(((bf16[2,4,256,1792]{2,3,0,1:T(8,128)(2,1)}), bf16[2,4,256,1792]{2,3,0,1:T(8,128)(2,1)}, u32[]{:S(2)}, u32[]{:S(2)}) %all-to-all-start) | async-done | bytes 7340064 | tf_op jit(solution)/shard_map/all_to_all | solution.py:142
  111.6 3.6 copy.51
  115.2 47.2 %copy.52 = bf16[2,1,256,7168]{2,0,1,3:T(2,128)(2,1)} copy(bf16[2,1,256,7168]{2,3,0,1:T(8,128)(2,1)S(1)} %bitcast.73) | data formatting | bytes 14680064 | tf_op jit(solution)/shard_map/all_to_all | solution.py:142
  162.3 7.7 %all-to-all-start.1 = ((bf16[2,1,256,7168]{2,0,1,3:T(2,128)(2,1)}), bf16[2,1,256,7168]{2,0,1,3:T(2,128)(2,1)}, u32[]{:S(2)}, u32[]{:S(2)}) async-start(bf16[2,1,256,7168]{2,0,1,3:T(2,128)(2,1)} %copy.52), calls=%async_computation.1 | async-start | bytes 14680064 | tf_op jit(solution)/shard_map/all_to_all | solution.py:141
  170.0 106.1 %all-gather.6.cloned.1.call-done = bf16[1,2048,1792]{1,2,0:T(8,128)(2,1)} async-done(((bf16[1,256,1792]{1,2,0:T(8,128)(2,1)}), bf16[1,2048,1792]{1,2,0:T(8,128)(2,1)}) %all-gather.6.cloned.1.call-update) | async-done | bytes 7340048 | tf_op jit(solution)/shard_map/all_gather | solution.py:115
  276.2 51.9 %while.18 = (s32[]{:T(128)}, f32[8,256]{1,0:T(8,128)S(1)}, f32[8,256]{1,0:T(8,128)S(1)}, f32[8,256,224]{1,2,0:T(8,128)}, s32[4]{0:T(128)S(1)}, /*index=5*/s32[25...) while((s32[]{:T(128)}, f32[8,256]{1,0:T(8,128)S(1)}, ...), condition=%wide.region_8.9_spmd.clone, body=%wide.region_4.8_spmd.clone.sunk | while | flops 955204608 | bytes 45631228 | solution.py:131
  276.6 2.3 constant_dynamic-slice_fusion.3
  278.9 3.1 fusion.45
  281.9 3.3 fusion.46
  285.4 2.6 fusion.48
  288.4 2.3 constant_dynamic-slice_fusion.3
  290.7 3.1 fusion.45
  293.8 3.3 fusion.46
  297.2 4.1 %fusion.48 = f32[8,256,224]{1,2,0:T(8,128)} fusion(f32[8,256,224]{1,2,0:T(8,128)} %get-tuple-element.350, bf16[512,8,224]{0,2,1:T(8,128)(2,1)S(1)} %bitcast.71, f32[8,512,256]{2,1,0:T(8,128)S(1)} %copy-done, f32[8,256]{1,0:T(8,128)S(1)} %select_maximum_fusion.2, pred[256,512]{0,1:T(8,128)(4,1)S(1)} %and_or_fusion.2, ...), kind=kOutput, calls=%fused_computation.13.clone.1 | convolution fusion | flops 476381184 | bytes 9846785 | tf_op jit(solution)/shard_map/while/body/eval_jaxpr/eva,ael->evl/dot_general | solution.py:85
  301.8 2.3 constant_dynamic-slice_fusion.3
  304.1 3.1 fusion.45
  307.2 3.3 fusion.46
  310.6 4.1 %fusion.48 = f32[8,256,224]{1,2,0:T(8,128)} fusion(f32[8,256,224]{1,2,0:T(8,128)} %get-tuple-element.350, bf16[512,8,224]{0,2,1:T(8,128)(2,1)S(1)} %bitcast.71, f32[8,512,256]{2,1,0:T(8,128)S(1)} %copy-done, f32[8,256]{1,0:T(8,128)S(1)} %select_maximum_fusion.2, pred[256,512]{0,1:T(8,128)(4,1)S(1)} %and_or_fusion.2, ...), kind=kOutput, calls=%fused_computation.13.clone.1 | convolution fusion | flops 476381184 | bytes 9846785 | tf_op jit(solution)/shard_map/while/body/eval_jaxpr/eva,ael->evl/dot_general | solution.py:85
  315.1 2.3 constant_dynamic-slice_fusion.3
  317.4 3.1 fusion.45
  320.5 3.3 fusion.46
  323.9 4.1 %fusion.48 = f32[8,256,224]{1,2,0:T(8,128)} fusion(f32[8,256,224]{1,2,0:T(8,128)} %get-tuple-element.350, bf16[512,8,224]{0,2,1:T(8,128)(2,1)S(1)} %bitcast.71, f32[8,512,256]{2,1,0:T(8,128)S(1)} %copy-done, f32[8,256]{1,0:T(8,128)S(1)} %select_maximum_fusion.2, pred[256,512]{0,1:T(8,128)(4,1)S(1)} %and_or_fusion.2, ...), kind=kOutput, calls=%fused_computation.13.clone.1 | convolution fusion | flops 476381184 | bytes 9846785 | tf_op jit(solution)/shard_map/while/body/eval_jaxpr/eva,ael->evl/dot_general | solution.py:85
  328.1 1.6 divide_convert_fusion
  331.1 24.2 %all-to-all-done.1 = bf16[2,1,256,7168]{2,0,1,3:T(2,128)(2,1)} async-done(((bf16[2,1,256,7168]{2,0,1,3:T(2,128)(2,1)}), bf16[2,1,256,7168]{2,0,1,3:T(2,128)(2,1)}, u32[]{:S(2)}, u32[]{:S(2)}) %all-to-all-start.1) | async-done | bytes 7340064 | tf_op jit(solution)/shard_map/all_to_all | solution.py:141
  355.3 7.0 %copy.53 = bf16[2,1,256,7168]{2,3,0,1:T(8,128)(2,1)} copy(bf16[2,1,256,7168]{2,0,1,3:T(2,128)(2,1)} %all-to-all-done.1) | data formatting | bytes 14680064 | tf_op jit(solution)/shard_map/all_to_all | solution.py:141
  362.3 11.1 %copy.54 = bf16[2,1,8,256,896]{4,3,2,0,1:T(8,128)(2,1)} copy(bf16[2,1,8,256,896]{3,4,2,0,1:T(8,128)(2,1)} %bitcast.74) | data formatting | bytes 14680064 | tf_op jit(solution)/shard_map/all_to_all | solution.py:141
  373.4 5.6 %fusion.19 = (bf16[1,1,1024,896]{3,2,1,0:T(8,128)(2,1)}, bf16[1,1,1024,896]{3,2,1,0:T(8,128)(2,1)}) fusion(s32[]{:T(128)S(6)} %add.111, s32[]{:T(128)S(6)} %select_n.53, bf16[2,1,2048,896]{3,2,0,1:T(8,128)(2,1)} %bitcast.75), kind=kLoop, calls=%fused_computation.32 | loop fusion | bytes 11010056
  (81 shorter events, 12.4 us)
Async XLA Ops:
  7.2 5.8 %copy-start.2 = (bf16[1,256,1792]{2,1,0:T(8,128)(2,1)S(1)}, bf16[1,256,1792]{2,1,0:T(8,128)(2,1)}, u32[]{:S(2)}) copy-start(bf16[1,256,1792]{2,1,0:T(8,128)(2,1)} %param.10) | copy-start | bytes 2752516
  7.2 162.8 %all-gather.4.cloned.1.call-start = ((), (), s32[]{:S(2)}) async-start(), calls=%async_computation.2 | async-start | bytes 8257536 | tf_op jit(solution)/shard_map/all_gather | solution.py:114
  12.9 1.4 copy-start.1
  12.9 263.2 %all-gather.6.cloned.1.call-start = ((), (), s32[]{:S(2)}) async-start(), calls=%async_computation.3 | async-start | bytes 8257536 | tf_op jit(solution)/shard_map/all_gather | solution.py:115
  22.6 5.6 %copy-start.3 = (bf16[1,256,1792]{2,1,0:T(8,128)(2,1)S(1)}, bf16[1,256,1792]{2,1,0:T(8,128)(2,1)}, u32[]{:S(2)}) copy-start(bf16[1,256,1792]{2,1,0:T(8,128)(2,1)} %param.8) | copy-start | bytes 2752516
  22.6 6.2 %copy-start.5 = (s32[1,4]{1,0:T(1,128)S(1)}, s32[1,4]{1,0:T(1,128)}, u32[]{:S(2)}) copy-start(s32[1,4]{1,0:T(1,128)} %param.13) | copy-start | bytes 52
  22.6 6.9 %copy-start.4 = (s32[1,4]{1,0:T(1,128)S(1)}, s32[1,4]{1,0:T(1,128)}, u32[]{:S(2)}) copy-start(s32[1,4]{1,0:T(1,128)} %param.11) | copy-start | bytes 52
  22.6 89.0 %all-to-all-start = ((bf16[2,4,256,1792]{2,3,0,1:T(8,128)(2,1)}), bf16[2,4,256,1792]{2,3,0,1:T(8,128)(2,1)}, u32[]{:S(2)}, u32[]{:S(2)}) async-start(bf16[2,4,256,1792]{2,3,0,1:T(8,128)(2,1)} %broadcast_select_fusion), calls=%async_computation | async-start | bytes 14680064 | tf_op jit(solution)/shard_map/all_to_all | solution.py:142
  162.3 192.9 %all-to-all-start.1 = ((bf16[2,1,256,7168]{2,0,1,3:T(2,128)(2,1)}), bf16[2,1,256,7168]{2,0,1,3:T(2,128)(2,1)}, u32[]{:S(2)}, u32[]{:S(2)}) async-start(bf16[2,1,256,7168]{2,0,1,3:T(2,128)(2,1)} %copy.52), calls=%async_computation.1 | async-start | bytes 14680064 | tf_op jit(solution)/shard_map/all_to_all | solution.py:141
  281.9 3.4 copy-start
  293.8 3.4 copy-start
  307.1 3.4 copy-start
  320.5 3.4 copy-start
Sparse Core Ops, SparseCore 0:
  13.1 91.4 all-gather.3
  106.8 169.2 all-gather.5
where the time goes:
time: 387 us; the launch traced here: 386 us
  waiting for transfers between devices  209 us (54%)
  local copies, waits for them, and re-layouts  92 us (24%)
  other arithmetic  28 us (7%)
  matrix products  27.3 us (7%)
  between operations  16.1 us (4%)
  starting transfers between devices  13.3 us (3%)
    all_gather x1, waiting for transfers between devices, per_device(): piece_values = lax.all_gather(value_rows, 'seq', axis=0, tiled=True)  106 us
    all_to_all x1, waiting for transfers between devices, per_device(): lax.all_to_all(buckets, 'head', split_axis=1, concat_axis=3, tiled=True)  78.6 us
    all_to_all x2, local copies, waits for them, and re-layouts, per_device(): lax.all_to_all(buckets, 'head', split_axis=1, concat_axis=3, tiled=True)  50.7 us
    all_to_all x1, waiting for transfers between devices, per_device(): lax.all_to_all(lax.all_to_all(buckets, 'head', split_axis=1, concat_axis=...  24.2 us
    all_to_all x2, local copies, waits for them, and re-layouts, per_device(): lax.all_to_all(lax.all_to_all(buckets, 'head', split_axis=1, concat_axis=...  18.1 us
    dot_general x4, matrix products, update(): jnp.einsum('eva,ael->evl', weights.astype(jnp.bfloat16), value_heads, pre...  15 us
    reduce_sum x4, other arithmetic, update(): total_new = row_total * factor + jnp.sum(weights, axis=2)  13.3 us
    dot_general x4, matrix products, update(): jnp.einsum('ezq,izq->zei', query_token_rows, key_head_stack, preferred_el...  12.3 us
  transfers between devices with their start and end apart: 4, of which 3 were waited for; matrix products, arithmetic and copies ran while one was open for 31% of the time, Pallas kernels for 0%

commit v1 on v0

--- a/solution.py
+++ b/solution.py
@@ -112,7 +112,21 @@
     )
     value_rows = new_values[0]
     key_rows = lax.all_gather(rot_keys, "seq", axis=0, tiled=True)
-    piece_values = lax.all_gather(value_rows, "seq", axis=0, tiled=True)
+    ways, here, step = (lax.axis_size("seq"), lax.axis_index("seq"), value_rows.shape[0])
+    shape = [n * ways if d == 0 else n for d, n in enumerate(value_rows.shape)]
+    full = lax.dynamic_update_slice_in_dim(
+        jnp.zeros(shape, value_rows.dtype), value_rows, here * step, axis=0
+    )
+    going_up = going_down = value_rows
+    for far in range(1, ways // 2 + 1):
+        going_up = lax.ppermute(going_up, "seq", [(d, (d + 1) % ways) for d in range(ways)])
+        full = lax.dynamic_update_slice_in_dim(full, going_up, (here - far) % ways * step, axis=0)
+        if 2 * far < ways:
+            going_down = lax.ppermute(going_down, "seq", [(d, (d - 1) % ways) for d in range(ways)])
+            full = lax.dynamic_update_slice_in_dim(
+                full, going_down, (here + far) % ways * step, axis=0
+            )
+    piece_values = full
     row_count = key_rows.shape[0]
 
     def key_step(key_index, state_in):

time: 387 us -> 432 us (1.12)
  the two profiles are of different devices: /device:TPU:96 before, /device:TPU:1 now
where the time goes in v1:
time: 432 us; the launch traced here: 431 us
  waiting for transfers between devices  225 us (52%)
  local copies, waits for them, and re-layouts  109 us (25%)
  other arithmetic  28.7 us (7%)
  matrix products  27.3 us (6%)
  starting transfers between devices  24.4 us (6%)
  between operations  16.2 us (4%)
    ppermute x4, waiting for transfers between devices, per_device(): lax.ppermute(going_up, 'seq', [(d, (d + 1) % ways) for d in range(ways)])  115 us
    all_to_all x1, waiting for transfers between devices, per_device(): lax.all_to_all(lax.all_to_all(buckets, 'head', split_axis=1, concat_axis=...  109 us
    all_to_all x2, local copies, waits for them, and re-layouts, per_device(): lax.all_to_all(buckets, 'head', split_axis=1, concat_axis=3, tiled=True)  50.7 us
    all_to_all x2, local copies, waits for them, and re-layouts, per_device(): lax.all_to_all(lax.all_to_all(buckets, 'head', split_axis=1, concat_axis=...  18.1 us
    dot_general x4, matrix products, update(): jnp.einsum('eva,ael->evl', weights.astype(jnp.bfloat16), value_heads, pre...  15 us
    reduce_sum x4, other arithmetic, update(): total_new = row_total * factor + jnp.sum(weights, axis=2)  13.3 us
    dot_general x4, matrix products, update(): jnp.einsum('ezq,izq->zei', query_token_rows, key_head_stack, preferred_el...  12.3 us
    unnamed x13, local copies, waits for them, and re-layouts  10.5 us
  transfers between devices with their start and end apart: 10, of which 5 were waited for; matrix products, arithmetic and copies ran while one was open for 31% of the time, Pallas kernels for 0%

profile of v1, /device:TPU:1, one launch (start us, length us, event | category | flops | bytes accessed | tf_op | source)
XLA Modules:
  0.0 430.5 jit_solution(17978324677844821165)
XLA Ops:
  15.8 2.8 copy.50
  18.6 3.4 broadcast_select_fusion
  22.0 8.8 %all-to-all-start = ((bf16[2,4,256,1792]{2,3,0,1:T(8,128)(2,1)}), bf16[2,4,256,1792]{2,3,0,1:T(8,128)(2,1)}, u32[]{:S(2)}, u32[]{:S(2)}) async-start(bf16[2,4,256,1792]{2,3,0,1:T(8,128)(2,1)} %broadcast_select_fusion), calls=%async_computation | async-start | bytes 14680064 | tf_op jit(solution)/shard_map/all_to_all | solution.py:156
  31.5 4.0 collective-permute-start.1
  35.5 35.9 %collective-permute-done = bf16[256,1792]{0,1:T(8,128)(2,1)} collective-permute-done((bf16[256,1792]{0,1:T(8,128)(2,1)S(1)}, bf16[256,1792]{0,1:T(8,128)(2,1)}, u32[]{:S(2)}, u32[]{:S(2)}) %collective-permute-start) | collective-permute-done | bytes 917536 | tf_op jit(solution)/shard_map/ppermute | solution.py:122
  73.8 2.7 collective-permute-start.3
  80.8 29.6 %collective-permute-done.2 = bf16[256,1792]{0,1:T(8,128)(2,1)} collective-permute-done((bf16[256,1792]{0,1:T(8,128)(2,1)}, bf16[256,1792]{0,1:T(8,128)(2,1)}, u32[]{:S(2)}, u32[]{:S(2)}) %collective-permute-start.2) | collective-permute-done | bytes 917536 | tf_op jit(solution)/shard_map/ppermute | solution.py:122
  111.7 3.9 broadcast_in_dim.165
  122.5 26.6 %collective-permute-done.4 = bf16[256,1792]{0,1:T(8,128)(2,1)S(1)} collective-permute-done((bf16[256,1792]{0,1:T(8,128)(2,1)}, bf16[256,1792]{0,1:T(8,128)(2,1)S(1)}, u32[]{:S(2)}, u32[]{:S(2)}) %collective-permute-start.4) | collective-permute-done | bytes 917536 | tf_op jit(solution)/shard_map/ppermute | solution.py:122
  155.7 23.3 %collective-permute-done.6 = bf16[256,1792]{0,1:T(8,128)(2,1)S(1)} collective-permute-done((bf16[256,1792]{0,1:T(8,128)(2,1)S(1)}, bf16[256,1792]{0,1:T(8,128)(2,1)S(1)}, u32[]{:S(2)}, u32[]{:S(2)}) %collective-permute-start.6) | collective-permute-done | bytes 917536 | tf_op jit(solution)/shard_map/ppermute | solution.py:122
  180.0 3.6 copy.51
  183.6 47.2 %copy.52 = bf16[2,1,256,7168]{2,0,1,3:T(2,128)(2,1)} copy(bf16[2,1,256,7168]{2,3,0,1:T(8,128)(2,1)S(1)} %bitcast.74) | data formatting | bytes 14680064 | tf_op jit(solution)/shard_map/all_to_all | solution.py:156
  230.7 5.0 %all-to-all-start.1 = ((bf16[2,1,256,7168]{2,0,1,3:T(2,128)(2,1)}), bf16[2,1,256,7168]{2,0,1,3:T(2,128)(2,1)}, u32[]{:S(2)}, u32[]{:S(2)}) async-start(bf16[2,1,256,7168]{2,0,1,3:T(2,128)(2,1)} %copy.52), calls=%async_computation.1 | async-start | bytes 14680064 | tf_op jit(solution)/shard_map/all_to_all | solution.py:155
  235.8 52.0 %while.18 = (s32[]{:T(128)}, f32[8,256]{1,0:T(8,128)S(1)}, f32[8,256]{1,0:T(8,128)S(1)}, f32[8,256,224]{1,2,0:T(8,128)}, s32[4]{0:T(128)S(1)}, /*index=5*/s32[25...) while((s32[]{:T(128)}, f32[8,256]{1,0:T(8,128)S(1)}, ...), condition=%wide.region_8.9_spmd.clone, body=%wide.region_4.8_spmd.clone.sunk | while | flops 955204608 | bytes 45631220 | solution.py:145
  236.2 2.3 constant_dynamic-slice_fusion.3
  238.5 3.1 fusion.45
  241.6 3.3 fusion.46
  245.0 2.6 fusion.48
  250.4 3.1 fusion.45
  253.4 3.3 fusion.46
  256.9 4.1 fusion.48
  261.4 2.3 constant_dynamic-slice_fusion.3
  263.7 3.1 fusion.45
  266.8 3.3 fusion.46
  270.3 4.1 fusion.48
  277.1 3.1 fusion.45
  280.2 3.3 fusion.46
  283.6 4.1 fusion.48
  290.8 109.2 %all-to-all-done.1 = bf16[2,1,256,7168]{2,0,1,3:T(2,128)(2,1)} async-done(((bf16[2,1,256,7168]{2,0,1,3:T(2,128)(2,1)}), bf16[2,1,256,7168]{2,0,1,3:T(2,128)(2,1)}, u32[]{:S(2)}, u32[]{:S(2)}) %all-to-all-start.1) | async-done | bytes 7340064 | tf_op jit(solution)/shard_map/all_to_all | solution.py:155
  400.0 7.0 %copy.53 = bf16[2,1,256,7168]{2,3,0,1:T(8,128)(2,1)} copy(bf16[2,1,256,7168]{2,0,1,3:T(2,128)(2,1)} %all-to-all-done.1) | data formatting | bytes 14680064 | tf_op jit(solution)/shard_map/all_to_all | solution.py:155
  407.0 11.1 %copy.54 = bf16[2,1,8,256,896]{4,3,2,0,1:T(8,128)(2,1)} copy(bf16[2,1,8,256,896]{3,4,2,0,1:T(8,128)(2,1)} %bitcast.75) | data formatting | bytes 14680064 | tf_op jit(solution)/shard_map/all_to_all | solution.py:155
  418.1 5.6 %fusion.19 = (bf16[1,1,1024,896]{3,2,1,0:T(8,128)(2,1)}, bf16[1,1,1024,896]{3,2,1,0:T(8,128)(2,1)}) fusion(s32[]{:T(128)S(6)} %add.188, s32[]{:T(128)S(6)} %select_n.123, bf16[2,1,2048,896]{3,2,0,1:T(8,128)(2,1)} %bitcast.76), kind=kLoop, calls=%fused_computation.32 | loop fusion | bytes 11010056
  (99 shorter events, 39.2 us)
Async XLA Ops:
  7.2 228.6 %all-gather.2.cloned.1.call-start = ((), (), s32[]{:S(2)}) async-start(), calls=%async_computation.2 | async-start | bytes 8257536 | tf_op jit(solution)/shard_map/all_gather | solution.py:114
  8.7 5.7 %copy-start.1 = (bf16[1,256,1792]{2,1,0:T(8,128)(2,1)S(1)}, bf16[1,256,1792]{2,1,0:T(8,128)(2,1)}, u32[]{:S(2)}) copy-start(bf16[1,256,1792]{2,1,0:T(8,128)(2,1)} %param.10) | copy-start | bytes 2752516
  22.0 50.8 %copy-start.4 = (s32[1,4]{1,0:T(1,128)S(1)}, s32[1,4]{1,0:T(1,128)}, u32[]{:S(2)}) copy-start(s32[1,4]{1,0:T(1,128)} %param.13) | copy-start | bytes 52
  22.0 157.9 %all-to-all-start = ((bf16[2,4,256,1792]{2,3,0,1:T(8,128)(2,1)}), bf16[2,4,256,1792]{2,3,0,1:T(8,128)(2,1)}, u32[]{:S(2)}, u32[]{:S(2)}) async-start(bf16[2,4,256,1792]{2,3,0,1:T(8,128)(2,1)} %broadcast_select_fusion), calls=%async_computation | async-start | bytes 14680064 | tf_op jit(solution)/shard_map/all_to_all | solution.py:156
  30.9 45.7 %copy-start.3 = (s32[1,4]{1,0:T(1,128)S(1)}, s32[1,4]{1,0:T(1,128)}, u32[]{:S(2)}) copy-start(s32[1,4]{1,0:T(1,128)} %param.11) | copy-start | bytes 52
  31.4 40.0 %collective-permute-start = (bf16[256,1792]{0,1:T(8,128)(2,1)S(1)}, bf16[256,1792]{0,1:T(8,128)(2,1)}, u32[]{:S(2)}, u32[]{:S(2)}) collective-permute-start(bf16[256,1792]{0,1:T(8,128)(2,1)S(1)} %bitcast.79), channel_id=1, source_target_pairs={{0,32},{32,64},{64,96},{96,128},{128,160},{160,192},{192,224},{224... | collective-permute-start | bytes 2752520 | tf_op jit(solution)/shard_map/ppermute | solution.py:122
  31.5 42.3 %collective-permute-start.1 = (bf16[256,1792]{0,1:T(8,128)(2,1)S(1)}, bf16[256,1792]{0,1:T(8,128)(2,1)}, u32[]{:S(2)}, u32[]{:S(2)}) collective-permute-start(bf16[256,1792]{0,1:T(8,128)(2,1)S(1)} %bitcast.80), channel_id=1, source_target_pairs={{0,224},{32,0},{64,32},{96,64},{128,96},{160,128},{192,160},{224,1... | collective-permute-start | bytes 2752520 | tf_op jit(solution)/shard_map/ppermute | solution.py:125
  71.4 39.1 %collective-permute-start.2 = (bf16[256,1792]{0,1:T(8,128)(2,1)}, bf16[256,1792]{0,1:T(8,128)(2,1)}, u32[]{:S(2)}, u32[]{:S(2)}) collective-permute-start(bf16[256,1792]{0,1:T(8,128)(2,1)} %collective-permute-done), channel_id=1, source_target_pairs={{0,32},{32,64},{64,96},{96,128},{128,160},{160,192},{192,224},{224... | collective-permute-start | bytes 2752520 | tf_op jit(solution)/shard_map/ppermute | solution.py:122
  73.8 45.0 %collective-permute-start.3 = (bf16[256,1792]{0,1:T(8,128)(2,1)}, bf16[256,1792]{0,1:T(8,128)(2,1)S(1)}, u32[]{:S(2)}, u32[]{:S(2)}) collective-permute-start(bf16[256,1792]{0,1:T(8,128)(2,1)} %collective-permute-done.1), channel_id=1, source_target_pairs={{0,224},{32,0},{64,32},{96,64},{128,96},{160,128},{192,160},{224,1... | collective-permute-start | bytes 2752520 | tf_op jit(solution)/shard_map/ppermute | solution.py:125
  110.4 38.7 %collective-permute-start.4 = (bf16[256,1792]{0,1:T(8,128)(2,1)}, bf16[256,1792]{0,1:T(8,128)(2,1)S(1)}, u32[]{:S(2)}, u32[]{:S(2)}) collective-permute-start(bf16[256,1792]{0,1:T(8,128)(2,1)} %collective-permute-done.2), channel_id=1, source_target_pairs={{0,32},{32,64},{64,96},{96,128},{128,160},{160,192},{192,224},{224... | collective-permute-start | bytes 2752520 | tf_op jit(solution)/shard_map/ppermute | solution.py:122
  118.8 35.8 %collective-permute-start.5 = (bf16[256,1792]{0,1:T(8,128)(2,1)S(1)}, bf16[256,1792]{0,1:T(8,128)(2,1)S(1)}, u32[]{:S(2)}, u32[]{:S(2)}) collective-permute-start(bf16[256,1792]{0,1:T(8,128)(2,1)S(1)} %collective-permute-done.3), channel_id=1, source_target_pairs={{0,224},{32,0},{64,32},{96,64},{128,96},{160,128},{192,160},{224,1... | collective-permute-start | bytes 2752520 | tf_op jit(solution)/shard_map/ppermute | solution.py:125
  149.1 29.8 %collective-permute-start.6 = (bf16[256,1792]{0,1:T(8,128)(2,1)S(1)}, bf16[256,1792]{0,1:T(8,128)(2,1)S(1)}, u32[]{:S(2)}, u32[]{:S(2)}) collective-permute-start(bf16[256,1792]{0,1:T(8,128)(2,1)S(1)} %collective-permute-done.4), channel_id=1, source_target_pairs={{0,32},{32,64},{64,96},{96,128},{128,160},{160,192},{192,224},{224... | collective-permute-start | bytes 2752520 | tf_op jit(solution)/shard_map/ppermute | solution.py:122
  230.7 5.0 %copy-start.2 = (bf16[256,8,224]{0,2,1:T(8,128)(2,1)S(1)}, bf16[256,8,224]{0,2,1:T(8,128)(2,1)}, u32[]{:S(2)}) copy-start(bf16[256,8,224]{0,2,1:T(8,128)(2,1)} %pad_maximum_fusion.1) | copy-start | bytes 2752516
  230.7 169.3 %all-to-all-start.1 = ((bf16[2,1,256,7168]{2,0,1,3:T(2,128)(2,1)}), bf16[2,1,256,7168]{2,0,1,3:T(2,128)(2,1)}, u32[]{:S(2)}, u32[]{:S(2)}) async-start(bf16[2,1,256,7168]{2,0,1,3:T(2,128)(2,1)} %copy.52), calls=%async_computation.1 | async-start | bytes 14680064 | tf_op jit(solution)/shard_map/all_to_all | solution.py:155
  241.6 3.4 copy-start
  253.4 3.4 copy-start
  266.8 3.4 copy-start
  280.2 3.4 copy-start
Sparse Core Ops, SparseCore 0:
  13.1 146.8 all-gather.1
